TPU v7x, 32 devices: a whole 2x2x4 slice. The times are simulated.
32 devices in a mesh: groups: 2 (over y), rows: 4 (over z), mp: 2 (over x), pair: 2 (over core).
Axes of the slice: x: 2, y: 2, z: 4, core: 2. Of those that a mesh axis runs over, the one named last changes fastest.
Arguments:
- query_rows: bfloat16 [2048, 512], P(('groups', 'rows', 'pair'), 'mp'), parts along dimension 0, may hold values from -240 to 240
- key_rows: bfloat16 [65536, 512], P(('groups', 'rows', 'pair'), 'mp'), parts along dimension 0, may hold values from -24 to 24
- value_rows: bfloat16 [65536, 512], P(('groups', 'rows', 'pair'), 'mp'), parts along dimension 0, may hold values from -6 to 6
- cotangent: bfloat16 [2048, 512], P(('groups', 'rows', 'pair'), 'mp'), parts along dimension 0, may hold values from -1536 to 1536
- train_rows: int32 [16], P('groups'), parts along dimension 0, may hold values from 1 to 12288, as said below
- test_rows: int32 [16], P('groups'), parts along dimension 0, may hold values from 32 to 128
- block_table: int32 [128], P('groups'), parts along dimension 0, may hold values from 0 to 7, as said below
Outputs:
- query_grad: bfloat16 [2048, 512], P(('groups', 'rows', 'pair'), 'mp'), parts along dimension 0
- key_grad: bfloat16 [65536, 512], P(('groups', 'rows', 'pair'), 'mp'), parts along dimension 0
- value_grad: bfloat16 [65536, 512], P(('groups', 'rows', 'pair'), 'mp'), parts along dimension 0
There are 2 independent parts, one for each index of `groups`. A program takes and returns all parts, laid end to end along the dimension named above; each array names one. Nothing has to cross between parts.
Inputs may be any that keep to these rules, and one draw needn't show every extreme that they name: block_table names table t exactly ceil(train_rows[t] / 512) times; the largest table has 24 full blocks. `block_table`: every table is named at least once.
All inputs are finite; a program needn't handle non-finite values.
Results may differ from a plain program's by a relative error of at most 0.0075.
Values may be sent and summed in bfloat16 or wider, within the bound.
No kernel may reach another device: no remote copies, remote signals or barrier semaphores. Data moves between devices by JAX's collectives and lax.ppermute only.
A program may use at most 64 MiB of HBM per device.

v0:
```python
import math
import jax
import jax.numpy as jnp
from jax import lax
from jax.sharding import PartitionSpec as P

HD = 64
TEST = 128
BLK = 512
NEG = -1e30


def combined_all(value, axis, join):
    pieces = jax.tree.map(lambda part: lax.all_gather(part, axis), value)
    head = jax.tree.map(lambda part: part[0], pieces)
    tail = jax.tree.map(lambda part: part[1:], pieces)
    total, _ = lax.scan(lambda total, piece: (join(total, piece), None), head, tail)
    return total


def table_lookup(positions, entries):
    matches = positions[:, None] == jnp.arange(entries.shape[0], dtype=jnp.int32)[None, :]
    return jnp.sum(jnp.where(matches, entries[None, :], 0), axis=1)


def merge_two(former, latter):
    new_peak = jnp.maximum(former[0], latter[0])
    return (
        new_peak,
        former[1] * jnp.exp(former[0] - new_peak) + latter[1] * jnp.exp(latter[0] - new_peak),
    )


def contract_rows(left, right):
    return lax.dot_general(
        left, right, (((0,), (0,)), ((), ())), preferred_element_type=jnp.float32
    )


def contract_features(left, right):
    return lax.dot_general(
        left, right, (((1,), (1,)), ((), ())), preferred_element_type=jnp.float32
    )


def local(query_rows, key_rows, value_rows, cotangent, train_rows, test_rows, block_table):
    device = lax.axis_index(("rows", "pair"))
    local_rows = query_rows.shape[0]
    features = query_rows.shape[1]
    head_count = features // HD
    blocks = key_rows.shape[0] // BLK
    tables = train_rows.shape[0]
    query_count = tables * TEST
    stacked = head_count * TEST
    score_scale = 1.0 / math.sqrt(HD)
    row_ids = device * local_rows + jnp.arange(local_rows, dtype=jnp.int32)
    query_live = row_ids % TEST < table_lookup(row_ids // TEST, test_rows)
    live_grads = jnp.where(query_live[:, None], cotangent, jnp.zeros_like(cotangent))
    all_queries, all_grads = (
        lax.all_gather(query_rows, ("rows", "pair"), axis=0, tiled=True),
        lax.all_gather(live_grads, ("rows", "pair"), axis=0, tiled=True),
    )
    head_of_feature = jnp.arange(features, dtype=jnp.int32) // HD
    head_mask = head_of_feature[None, :] == jnp.arange(head_count, dtype=jnp.int32)[:, None]

    def expand(rows):
        shaped = rows.reshape(tables, 1, TEST, features)
        masked = jnp.where(head_mask[None, :, None, :], shaped, jnp.zeros_like(shaped))
        return masked.reshape(tables, stacked, features)

    def collapse(product):
        shaped = product.reshape(head_count, TEST, features)
        return jnp.sum(jnp.where(head_mask[:, None, :], shaped, 0.0), axis=0)

    spread_queries = expand(all_queries)
    spread_grads = expand(all_grads)
    block_ids = jnp.arange(block_table.shape[0], dtype=jnp.int32)
    my_blocks = device * blocks + jnp.arange(blocks, dtype=jnp.int32)
    block_owner = lax.dynamic_slice_in_dim(block_table, device * blocks, blocks)
    earlier = (block_table[None, :] == block_owner[:, None]) & (
        block_ids[None, :] < my_blocks[:, None]
    )
    ordinal = jnp.sum(jnp.where(earlier, 1, 0), axis=1).astype(jnp.int32)
    live_keys = table_lookup(block_owner, train_rows) - ordinal * BLK
    key_blocks = key_rows.reshape(blocks, BLK, features)
    value_blocks = value_rows.reshape(blocks, BLK, features)
    key_index = jnp.arange(BLK, dtype=jnp.int32)
    block_inputs = (block_owner, live_keys, key_blocks, value_blocks)

    def block_scores(which_table, live_count, key_block):
        query_block = spread_queries[which_table]
        raw_scores = contract_features(query_block, key_block) * score_scale
        return (query_block, jnp.where(key_index[None, :] < live_count, raw_scores, NEG))

    def stats_step(running, inputs):
        which_table, live_count, key_block, value_block = inputs
        _, scores = block_scores(which_table, live_count, key_block)
        block_peak = jnp.max(scores, axis=1)
        weights = jnp.exp(scores - block_peak[:, None])
        block_mass = jnp.sum(weights, axis=1)
        old_peak = running[0][which_table]
        old_mass = running[1][which_table]
        new_peak = jnp.maximum(old_peak, block_peak)
        old_weight = jnp.exp(old_peak - new_peak)
        new_weight = jnp.exp(block_peak - new_peak)
        updated = [
            running[0].at[which_table].set(new_peak),
            running[1].at[which_table].set(old_mass * old_weight + block_mass * new_weight),
        ]
        return (tuple(updated), None)

    initial = [
        jnp.full((tables, stacked), NEG, jnp.float32),
        jnp.zeros((tables, stacked), jnp.float32),
    ]
    result, _ = lax.scan(stats_step, tuple(initial), block_inputs)
    peaks, masses = result
    peaks, masses = combined_all((peaks, masses), ("rows", "pair"), merge_two)

    def inner_step(running, inputs):
        which_table, live_count, key_block, value_block = inputs
        _, scores = block_scores(which_table, live_count, key_block)
        dprobs = contract_features(spread_grads[which_table], value_block)
        block_peak = jnp.max(scores, axis=1)
        weights_low = jnp.exp(scores - block_peak[:, None]).astype(jnp.bfloat16).astype(jnp.float32)
        term = (
            jnp.sum(weights_low * dprobs, axis=1)
            * jnp.exp(block_peak - peaks[which_table])
            / masses[which_table]
        )
        return (running.at[which_table].add(term), None)

    inner_terms, _ = lax.scan(inner_step, jnp.zeros((tables, stacked), jnp.float32), block_inputs)
    inner = lax.psum(inner_terms, ("rows", "pair"))

    def grad_step(running, inputs):
        which_table, live_count, key_block, value_block = inputs
        query_block, scores = block_scores(which_table, live_count, key_block)
        grad_block = spread_grads[which_table]
        probs = jnp.exp(scores - peaks[which_table][:, None]) / masses[which_table][:, None]
        dprobs = contract_features(grad_block, value_block)
        probs_low = probs.astype(jnp.bfloat16)
        value_part = contract_rows(probs_low, grad_block)
        dscores = (probs * (dprobs - inner[which_table][:, None])).astype(jnp.bfloat16)
        key_part = contract_rows(dscores, query_block) * score_scale
        query_part = (
            collapse(jnp.dot(dscores, key_block, preferred_element_type=jnp.float32)) * score_scale
        )
        running = running.at[which_table].add(query_part)
        return (running, (key_part.astype(jnp.bfloat16), value_part.astype(jnp.bfloat16)))

    query_terms, (key_parts, value_parts) = lax.scan(
        grad_step, jnp.zeros((tables, TEST, features), jnp.float32), block_inputs
    )
    query_total = lax.psum_scatter(
        query_terms.reshape(query_count, features),
        ("rows", "pair"),
        scatter_dimension=0,
        tiled=True,
    )
    return (
        query_total.astype(jnp.bfloat16),
        key_parts.reshape(blocks * BLK, features),
        value_parts.reshape(blocks * BLK, features),
    )


def solution(mesh):
    in_specs = (
        P(("groups", "rows", "pair"), "mp"),
        P(("groups", "rows", "pair"), "mp"),
        P(("groups", "rows", "pair"), "mp"),
        P(("groups", "rows", "pair"), "mp"),
        P("groups"),
        P("groups"),
        P("groups"),
    )
    out_specs = (
        P(("groups", "rows", "pair"), "mp"),
        P(("groups", "rows", "pair"), "mp"),
        P(("groups", "rows", "pair"), "mp"),
    )
    return jax.shard_map(local, mesh=mesh, in_specs=in_specs, out_specs=out_specs, check_vma=False)
```

profile of v0, /device:TPU:0, one launch (start us, length us, event | category | flops | bytes accessed | tf_op | source)
XLA Modules:
  0.0 357.1 jit_solution(11898617688526695184)
XLA Ops:
  11.4 16.6 %all_gather.23 = bf16[1024,256]{1,0:T(8,128)(2,1)S(1)} all-gather(bf16[128,256]{1,0:T(8,128)(2,1)S(1)} %broadcast_select_fusion.3), channel_id=1, replica_groups=mesh['groups'=2,'rows'=4,'mp'=2,'pair'=2] {'rows','pair'}, dimensions={0}, use_global_device_ids=true | all-gather | bytes 589824 | tf_op jit(solution)/shard_map/all_gather | solution.py:61
  28.0 14.9 %all_gather.18 = bf16[1024,256]{1,0:T(8,128)(2,1)S(1)} all-gather(bf16[128,256]{1,0:T(8,128)(2,1)} %param.23), channel_id=1, replica_groups=mesh['groups'=2,'rows'=4,'mp'=2,'pair'=2] {'rows','pair'}, dimensions={0}, use_global_device_ids=true | all-gather | bytes 589824 | tf_op jit(solution)/shard_map/all_gather | solution.py:60
  42.9 1.7 bitcast_select_fusion
  44.6 55.1 %while.60 = (s32[]{:T(128)}, f32[8,512]{1,0:T(8,128)S(1)}, f32[8,512]{1,0:T(8,128)S(1)}, s32[8]{0:T(128)S(1)}, s32[8]{0:T(128)S(1)}, /*index=5*/bf16[8,512,256]{...) while((s32[]{:T(128)}, f32[8,512]{1,0:T(8,128)S(1)}, ...), condition=%wide.region_7.8_spmd.clone.clone, body=%wide.region_3.7_spmd.clone.sunk.clone | while | flops 135532048 | bytes 2649797 | solution.py:116
  99.8 14.2 %all-gather.1 = f32[64,512]{1,0:T(8,128)S(1)} all-gather(f32[8,512]{1,0:T(8,128)S(1)} %get-tuple-element.259), channel_id=3, replica_groups=mesh['groups'=2,'rows'=4,'mp'=2,'pair'=2] {'rows','pair'}, dimensions={0}, use_global_device_ids=true | all-gather | bytes 147456 | tf_op jit(solution)/shard_map/all_gather | solution.py:14
  114.0 14.0 %all-gather = f32[64,512]{1,0:T(8,128)S(1)} all-gather(f32[8,512]{1,0:T(8,128)S(1)} %get-tuple-element.258), channel_id=2, replica_groups=mesh['groups'=2,'rows'=4,'mp'=2,'pair'=2] {'rows','pair'}, dimensions={0}, use_global_device_ids=true | all-gather | bytes 147456 | tf_op jit(solution)/shard_map/all_gather | solution.py:14
  128.3 61.7 %while.61 = (s32[]{:T(128)}, f32[8,512]{1,0:T(8,128)S(1)}, s32[8]{0:T(128)S(1)}, s32[8]{0:T(128)S(1)}, bf16[8,512,256]{2,1,0:T(8,128)(2,1)}, /*index=5*/bf16[8,5...) while((s32[]{:T(128)}, f32[8,512]{1,0:T(8,128)S(1)}, ...), condition=%wide.region_14.15_spmd.clone.clone, body=%wide.region_10.14_spmd.clone.sunk.clone | while | flops 270534656 | bytes 3170525 | solution.py:133
  190.1 29.2 %psum.7 = f32[8,512]{1,0:T(8,128)S(1)} all-reduce(f32[8,512]{1,0:T(8,128)S(1)} %get-tuple-element.262), channel_id=1, replica_groups=mesh['groups'=2,'rows'=4,'mp'=2,'pair'=2] {'rows','pair'}, use_global_device_ids=true, to_apply=%region_15.16 | all-reduce | flops 4096 | bytes 32768 | tf_op jit(solution)/shard_map/psum | solution.py:134
  219.4 97.7 %while.62 = (s32[]{:T(128)}, f32[8,128,256]{2,1,0:T(8,128)S(1)}, bf16[8,512,256]{2,1,0:T(8,128)(2,1)}, bf16[8,512,256]{2,1,0:T(8,128)(2,1)}, s32[8]{0:T(128)S(1)...) while((s32[]{:T(128)}, f32[8,128,256]{2,1,0:T(8,128)S(1)}, ...), condition=%wide.region_19.20_spmd.clone.clone, body=%wide.region_16.19_spmd.clone.sunk.clone | while | flops 673908224 | bytes 7627025 | solution.py:152
  229.6 2.0 fusion.131
  236.0 1.5 fusion.127
  241.8 2.0 fusion.131
  248.3 1.5 fusion.127
  254.0 2.0 fusion.131
  260.5 1.5 fusion.127
  266.2 2.0 fusion.131
  272.7 1.5 fusion.127
  278.4 2.0 fusion.131
  284.9 1.5 fusion.127
  290.6 2.0 fusion.131
  302.9 2.0 fusion.131
  315.1 2.0 fusion.131
  318.1 30.6 %reduce-scatter.2.cloned.1.call-done = f32[128,256]{1,0:T(8,128)} async-done(((f32[1024,256]{1,0:T(8,128)}), f32[128,256]{1,0:T(8,128)}) %reduce-scatter.2.cloned.1.call-update) | async-done | bytes 131088 | tf_op jit(solution)/shard_map/reduce_scatter | solution.py:155
  348.7 1.5 convert_element_type.21
  (265 shorter events, 151.3 us)
Async XLA Ops:
  7.2 341.5 %reduce-scatter.2.cloned.1.call-start = ((), (), s32[]{:S(2)}) async-start(), calls=%async_computation.1 | async-start | bytes 1179648 | tf_op jit(solution)/shard_map/reduce_scatter | solution.py:155
  42.9 1.7 copy-start.1
  128.3 91.1 %copy-start.2 = (s32[3]{0:T(128)S(1)}, s32[3]{0:T(128)}, u32[]{:S(2)}) copy-start(s32[3]{0:T(128)} %constant.200.clone.2) | copy-start | bytes 40
  317.1 1.0 copy-start
Sparse Core Ops, SparseCore 0:
  318.2 30.4 reduce-scatter.1
where the time goes:
time: 360 us; the launch traced here: 357 us
  matrix products  89.4 us (25%)
  blocking collectives  89 us (25%)
  other arithmetic  55.6 us (15%)
  loops' own time  45.8 us (13%)
  local copies, waits for them, and re-layouts  32.5 us (9%)
  waiting for transfers between devices  30.6 us (8%)
  between operations  14.2 us (4%)
    dot_general x40, matrix products, contract_features(): lax.dot_general(left, right, (((1,), (1,)), ((), ())), preferred_element_...  54.7 us
    reduce_scatter x1, waiting for transfers between devices, local(): lax.psum_scatter(query_terms.reshape(query_count, features), ('rows', 'pa...  30.6 us
    psum x1, blocking collectives, local(): inner = lax.psum(inner_terms, ('rows', 'pair'))  29.2 us
    dynamic_slice x48, local copies, waits for them, and re-layouts, local(): result, _ = lax.scan(stats_step, tuple(initial), block_inputs)  29 us
    all_gather x2, blocking collectives, combined_all(): pieces = jax.tree.map(lambda part: lax.all_gather(part, axis), value)  28.2 us
    another operation x42, other arithmetic  27.8 us
    dot_general x16, matrix products, contract_rows(): lax.dot_general(left, right, (((0,), (0,)), ((), ())), preferred_element_...  24.6 us
    all_gather x1, blocking collectives, local(): lax.all_gather(live_grads, ('rows', 'pair'), axis=0, tiled=True)  16.6 us
  transfers between devices with their start and end apart: 1, of which 1 were waited for; matrix products, arithmetic and copies ran while one was open for 0% of the time, Pallas kernels for 0%

commit v1 on v0

--- a/solution.py
+++ b/solution.py
@@ -131,7 +131,7 @@
         return (running.at[which_table].add(term), None)
 
     inner_terms, _ = lax.scan(inner_step, jnp.zeros((tables, stacked), jnp.float32), block_inputs)
-    inner = lax.psum(inner_terms, ("rows", "pair"))
+    inner = jnp.sum(lax.all_gather(inner_terms, ("rows", "pair")), axis=0)
 
     def grad_step(running, inputs):
         which_table, live_count, key_block, value_block = inputs

time: 360 us -> 348 us (0.967)
  blocking collectives: 89 us -> 73.7 us
    psum x1 -> x0, blocking collectives: 29.2 us -> none  [local(): inner = lax.psum(inner_terms, ('rows', 'pair'))]
    all_gather x0 -> x1, blocking collectives: none -> 14 us  [local(): inner = jnp.sum(lax.all_gather(inner_terms, ('rows', 'pair')), axis=0)]
where the time goes in v1:
time: 348 us; the launch traced here: 345 us
  matrix products  89.4 us (26%)
  blocking collectives  73.7 us (21%)
  other arithmetic  55.6 us (16%)
  loops' own time  45.8 us (13%)
  waiting for transfers between devices  33.7 us (10%)
  local copies, waits for them, and re-layouts  32.5 us (9%)
  between operations  14.2 us (4%)
    dot_general x40, matrix products, contract_features(): lax.dot_general(left, right, (((1,), (1,)), ((), ())), preferred_element_...  54.7 us
    reduce_scatter x1, waiting for transfers between devices, local(): lax.psum_scatter(query_terms.reshape(query_count, features), ('rows', 'pa...  33.7 us
    dynamic_slice x48, local copies, waits for them, and re-layouts, local(): result, _ = lax.scan(stats_step, tuple(initial), block_inputs)  29 us
    all_gather x2, blocking collectives, combined_all(): pieces = jax.tree.map(lambda part: lax.all_gather(part, axis), value)  28.2 us
    another operation x42, other arithmetic  27.8 us
    dot_general x16, matrix products, contract_rows(): lax.dot_general(left, right, (((0,), (0,)), ((), ())), preferred_element_...  24.6 us
    all_gather x1, blocking collectives, local(): lax.all_gather(live_grads, ('rows', 'pair'), axis=0, tiled=True)  16.6 us
    another operation x1, loops' own time, local(): result, _ = lax.scan(stats_step, tuple(initial), block_inputs)  15.3 us
  transfers between devices with their start and end apart: 1, of which 1 were waited for; matrix products, arithmetic and copies ran while one was open for 0% of the time, Pallas kernels for 0%

profile of v1, /device:TPU:0, one launch (start us, length us, event | category | flops | bytes accessed | tf_op | source)
XLA Modules:
  0.0 345.0 jit_solution(7053761417048738381)
XLA Ops:
  11.4 16.6 %all_gather.29 = bf16[1024,256]{1,0:T(8,128)(2,1)S(1)} all-gather(bf16[128,256]{1,0:T(8,128)(2,1)S(1)} %broadcast_select_fusion.3), channel_id=1, replica_groups=mesh['groups'=2,'rows'=4,'mp'=2,'pair'=2] {'rows','pair'}, dimensions={0}, use_global_device_ids=true | all-gather | bytes 589824 | tf_op jit(solution)/shard_map/all_gather | solution.py:61
  28.0 14.9 %all_gather.24 = bf16[1024,256]{1,0:T(8,128)(2,1)S(1)} all-gather(bf16[128,256]{1,0:T(8,128)(2,1)} %param.23), channel_id=1, replica_groups=mesh['groups'=2,'rows'=4,'mp'=2,'pair'=2] {'rows','pair'}, dimensions={0}, use_global_device_ids=true | all-gather | bytes 589824 | tf_op jit(solution)/shard_map/all_gather | solution.py:60
  42.9 1.7 bitcast_select_fusion
  44.6 55.1 %while.60 = (s32[]{:T(128)}, f32[8,512]{1,0:T(8,128)S(1)}, f32[8,512]{1,0:T(8,128)S(1)}, s32[8]{0:T(128)S(1)}, s32[8]{0:T(128)S(1)}, /*index=5*/bf16[8,512,256]{...) while((s32[]{:T(128)}, f32[8,512]{1,0:T(8,128)S(1)}, ...), condition=%wide.region_7.8_spmd.clone.clone, body=%wide.region_3.7_spmd.clone.sunk.clone | while | flops 135532048 | bytes 2649797 | solution.py:116
  99.8 14.2 %all-gather.1 = f32[64,512]{1,0:T(8,128)S(1)} all-gather(f32[8,512]{1,0:T(8,128)S(1)} %get-tuple-element.259), channel_id=3, replica_groups=mesh['groups'=2,'rows'=4,'mp'=2,'pair'=2] {'rows','pair'}, dimensions={0}, use_global_device_ids=true | all-gather | bytes 147456 | tf_op jit(solution)/shard_map/all_gather | solution.py:14
  114.0 14.0 %all-gather = f32[64,512]{1,0:T(8,128)S(1)} all-gather(f32[8,512]{1,0:T(8,128)S(1)} %get-tuple-element.258), channel_id=2, replica_groups=mesh['groups'=2,'rows'=4,'mp'=2,'pair'=2] {'rows','pair'}, dimensions={0}, use_global_device_ids=true | all-gather | bytes 147456 | tf_op jit(solution)/shard_map/all_gather | solution.py:14
  128.3 61.7 %while.61 = (s32[]{:T(128)}, f32[8,512]{1,0:T(8,128)S(1)}, s32[8]{0:T(128)S(1)}, s32[8]{0:T(128)S(1)}, bf16[8,512,256]{2,1,0:T(8,128)(2,1)}, /*index=5*/bf16[8,5...) while((s32[]{:T(128)}, f32[8,512]{1,0:T(8,128)S(1)}, ...), condition=%wide.region_14.15_spmd.clone.clone, body=%wide.region_10.14_spmd.clone.sunk.clone | while | flops 270534656 | bytes 3170525 | solution.py:133
  190.0 14.0 %all-gather.2 = f32[64,512]{1,0:T(8,128)S(1)} all-gather(f32[8,512]{1,0:T(8,128)S(1)} %get-tuple-element.262), channel_id=4, replica_groups=mesh['groups'=2,'rows'=4,'mp'=2,'pair'=2] {'rows','pair'}, dimensions={0}, use_global_device_ids=true | all-gather | bytes 147456 | tf_op jit(solution)/shard_map/all_gather | solution.py:134
  204.2 97.7 %while.62 = (s32[]{:T(128)}, f32[8,128,256]{2,1,0:T(8,128)S(1)}, bf16[8,512,256]{2,1,0:T(8,128)(2,1)}, bf16[8,512,256]{2,1,0:T(8,128)(2,1)}, s32[8]{0:T(128)S(1)...) while((s32[]{:T(128)}, f32[8,128,256]{2,1,0:T(8,128)S(1)}, ...), condition=%wide.region_19.20_spmd.clone.clone, body=%wide.region_16.19_spmd.clone.sunk.clone | while | flops 673908224 | bytes 7627025 | solution.py:152
  208.6 1.5 fusion.127
  214.4 2.0 fusion.131
  220.8 1.5 fusion.127
  226.6 2.0 fusion.131
  233.0 1.5 fusion.127
  238.8 2.0 fusion.131
  245.3 1.5 fusion.127
  251.0 2.0 fusion.131
  263.2 2.0 fusion.131
  269.7 1.5 fusion.127
  275.4 2.0 fusion.131
  287.7 2.0 fusion.131
  299.9 2.0 fusion.131
  302.9 33.7 %reduce-scatter.2.cloned.1.call-done = f32[128,256]{1,0:T(8,128)} async-done(((f32[1024,256]{1,0:T(8,128)}), f32[128,256]{1,0:T(8,128)}) %reduce-scatter.2.cloned.1.call-update) | async-done | bytes 131088 | tf_op jit(solution)/shard_map/reduce_scatter | solution.py:155
  336.6 1.5 convert_element_type.21
  (266 shorter events, 151.3 us)
Async XLA Ops:
  7.2 329.4 %reduce-scatter.2.cloned.1.call-start = ((), (), s32[]{:S(2)}) async-start(), calls=%async_computation.1 | async-start | bytes 1179648 | tf_op jit(solution)/shard_map/reduce_scatter | solution.py:155
  42.9 1.7 copy-start.1
  128.3 75.8 %copy-start.2 = (s32[3]{0:T(128)S(1)}, s32[3]{0:T(128)}, u32[]{:S(2)}) copy-start(s32[3]{0:T(128)} %constant.201.clone.2) | copy-start | bytes 40
  301.9 1.0 copy-start
Sparse Core Ops, SparseCore 0:
  303.0 33.5 reduce-scatter.1
